TPU v7x, 256 devices: a whole 4x4x8 slice. The times are simulated.
256 devices in a mesh: tensor: 8 (over z_hi, core), mirror: 2 (over z_lo), dp: 16 (over x, y).
Axes of the slice: x: 4, y: 4, z: 8 (z_hi: 4, z_lo: 2; z = z_hi * 2 + z_lo), core: 2. Of those that a mesh axis runs over, the one named last changes fastest.
Arguments:
- layer_input: bfloat16 [32, 256, 4096], P(('mirror', 'dp'), 'tensor'), may hold values from -6 to 6
- qk_weight: bfloat16 [4096, 2, 4096], P(None, None, 'tensor'), may hold values from -0.09375 to 0.09375
- query_proj: bfloat16 [32, 256, 4096], P(('mirror', 'dp'), None, 'tensor'), may hold values from -24 to 24
- key_proj: bfloat16 [32, 256, 4096], P(('mirror', 'dp'), None, 'tensor'), may hold values from -24 to 24
- value_proj: bfloat16 [32, 256, 4096], P(('mirror', 'dp'), None, 'tensor'), may hold values from -6 to 6
- head_grad: bfloat16 [32, 256, 4096], P(('mirror', 'dp'), None, 'tensor'), may hold values from -6 to 6
- doc_ids: int32 [32, 256], P(('mirror', 'dp')), may hold values from 0 to 3, as said below
Outputs:
- input_grad: bfloat16 [32, 256, 4096], P(('mirror', 'dp'), 'tensor')
- qk_weight_grad: float32 [4096, 2, 4096], P(('mirror', 'dp'), None, 'tensor')
Inputs may be any that keep to these rules, and one draw needn't show every extreme that they name: `doc_ids`: within each sequence of 128 tokens the ids start at 0, never fall, and each of the four documents holds a multiple of 8 tokens.
All inputs are finite; a program needn't handle non-finite values.
Results may differ from a plain program's by a relative error of at most 0.023.
Values may be sent and summed in bfloat16 or wider, within the bound.
A program may use at most 128 MiB of HBM per device.

v0:
```python
import math
import jax
import jax.numpy as jnp
from jax import lax
from jax.sharding import PartitionSpec as P

HD = 128
SEQ = 128


def rotate_pairs(values, cosine, sine_table):
    half = values.shape[-1] // 2
    first_half = values[..., :half]
    second_half = values[..., half:]
    cos_b = cosine[None, :, None, :]
    sin_b = sine_table[None, :, None, :]
    return jnp.concatenate(
        [first_half * cos_b - second_half * sin_b, second_half * cos_b + first_half * sin_b],
        axis=-1,
    )


def unrotate_pairs(values, cosine, sine_table):
    half = values.shape[-1] // 2
    first_half = values[..., :half]
    second_half = values[..., half:]
    cos_b = cosine[None, :, None, :]
    sin_b = sine_table[None, :, None, :]
    return jnp.concatenate(
        [first_half * cos_b + second_half * sin_b, second_half * cos_b - first_half * sin_b],
        axis=-1,
    )


def attention_grads(query_rows, key_rows, value_rows, grad_rows, doc_row):
    token_count, full_width = query_rows.shape
    head_count = full_width // HD
    micro_count = token_count // SEQ
    shape_four = (micro_count, SEQ, head_count, HD)
    positions = jnp.arange(SEQ).astype(jnp.float32)
    inverse = jnp.exp(-(2.0 * jnp.arange(HD // 2).astype(jnp.float32) / HD) * math.log(10000.0))
    angles = positions[:, None] * inverse[None, :]
    cosine = jnp.cos(angles)
    sine_table = jnp.sin(angles)
    q_rot = rotate_pairs(
        query_rows.reshape(shape_four).astype(jnp.float32), cosine, sine_table
    ).astype(jnp.bfloat16)
    k_rot = rotate_pairs(
        key_rows.reshape(shape_four).astype(jnp.float32), cosine, sine_table
    ).astype(jnp.bfloat16)
    scale = 1.0 / math.sqrt(HD)
    scores = jnp.einsum("bshd,bthd->bhst", q_rot, k_rot, preferred_element_type=jnp.float32) * scale
    docs = doc_row.reshape(micro_count, SEQ)
    index_seq = jnp.arange(SEQ)
    causal = index_seq[None, :] <= index_seq[:, None]
    allowed = causal[None, :, :] & (docs[:, :, None] == docs[:, None, :])
    scores = jnp.where(allowed[:, None, :, :], scores, -1e30)
    highest = jnp.max(scores, axis=-1, keepdims=True)
    exps = jnp.exp(scores - highest)
    probs = exps / jnp.sum(exps, axis=-1, keepdims=True)
    dprob = jnp.einsum(
        "bshd,bthd->bhst",
        grad_rows.reshape(shape_four),
        value_rows.reshape(shape_four),
        preferred_element_type=jnp.float32,
    )
    delta = jnp.sum(probs * dprob, axis=-1, keepdims=True)
    dscore = (probs * (dprob - delta)).astype(jnp.bfloat16)
    dq_rot = (
        jnp.einsum("bhst,bthd->bshd", dscore, k_rot, preferred_element_type=jnp.float32) * scale
    )
    dk_rot = (
        jnp.einsum("bhst,bshd->bthd", dscore, q_rot, preferred_element_type=jnp.float32) * scale
    )
    query_grad = (
        unrotate_pairs(dq_rot, cosine, sine_table)
        .astype(jnp.bfloat16)
        .reshape(token_count, full_width)
    )
    key_grad = (
        unrotate_pairs(dk_rot, cosine, sine_table)
        .astype(jnp.bfloat16)
        .reshape(token_count, full_width)
    )
    return (query_grad, key_grad)


def shards(layer_input, qk_weight, query_proj, key_proj, value_proj, head_grad, doc_ids):
    tensor_count = lax.axis_size("tensor")
    mirror_count = lax.axis_size("mirror")
    data_count = lax.axis_size("dp")
    replicas = mirror_count * data_count
    token_count = query_proj.shape[1]
    group_width = query_proj.shape[2]
    model_width = layer_input.shape[2]
    block_rows = model_width // replicas
    query_grad, key_grad = attention_grads(
        query_proj[0], key_proj[0], value_proj[0], head_grad[0], doc_ids[0]
    )
    grad_pair = jnp.concatenate([query_grad, key_grad], axis=1)
    weight_flat = qk_weight.reshape(model_width, 2 * group_width)
    summed_input = lax.psum_scatter(
        lax.dot_general(
            grad_pair, weight_flat, (((1,), (1,)), ((), ())), preferred_element_type=jnp.float32
        ).astype(jnp.bfloat16),
        "tensor",
        scatter_dimension=0,
        tiled=True,
    )
    input_grad = summed_input.reshape(1, token_count // tensor_count, model_width)
    gathered = lax.all_gather(layer_input, "tensor", axis=1, tiled=True)[0]
    summed = lax.psum_scatter(
        lax.dot_general(
            gathered, grad_pair, (((0,), (0,)), ((), ())), preferred_element_type=jnp.float32
        ).astype(jnp.bfloat16),
        ("mirror", "dp"),
        scatter_dimension=0,
        tiled=True,
    ).astype(jnp.float32)
    weight_grad = (summed / replicas).reshape(block_rows, 2, group_width)
    return (input_grad, weight_grad)


def solution(mesh):
    in_specs = (
        P(("mirror", "dp"), "tensor", None),
        P(None, None, "tensor"),
        P(("mirror", "dp"), None, "tensor"),
        P(("mirror", "dp"), None, "tensor"),
        P(("mirror", "dp"), None, "tensor"),
        P(("mirror", "dp"), None, "tensor"),
        P(("mirror", "dp"), None),
    )
    out_specs = (P(("mirror", "dp"), "tensor", None), P(("mirror", "dp"), None, "tensor"))
    return jax.shard_map(shards, mesh=mesh, in_specs=in_specs, out_specs=out_specs, check_vma=False)
```

profile of v0, /device:TPU:8, one launch (start us, length us, event | category | flops | bytes accessed | tf_op | source)
XLA Modules:
  0.0 301.0 jit_solution(3463841190845136703)
XLA Ops:
  7.2 0.0 all-gather.2.cloned.1.call-start
  7.2 0.7 all-gather.2.cloned.1.call-update
  7.9 0.0 reduce-scatter.7.cloned.1.call-start
  7.9 1.1 reshape.110
  9.1 1.1 reshape.111
  10.2 1.0 reshape_squeeze.9
  11.2 1.0 reshape_squeeze.8
  12.3 0.9 compare_and_fusion
  13.1 0.3 multiply_cosine_fusion
  13.4 0.6 fusion.18
  14.1 0.3 subtract_convert_fusion.3
  14.4 0.5 fusion.20
  14.9 0.3 multiply_reduce_fusion
  15.2 0.1 multiply_convert_fusion
  15.3 0.3 fusion.4
  15.6 0.4 fusion.5
  16.0 0.5 add_convert_fusion
  16.4 0.1 pad_maximum_fusion.2
  16.6 0.2 copy.42
  16.8 0.1 pad_maximum_fusion.3
  16.9 0.2 copy.46
  17.2 31.7 %all-gather.2.cloned.1.call-done = bf16[1,256,4096]{2,1,0:T(8,128)(2,1)} async-done(((bf16[1,32,4096]{2,1,0:T(8,128)(2,1)}), bf16[1,256,4096]{2,1,0:T(8,128)(2,1)}) %all-gather.2.cloned.1.call-update) | async-done | bytes 2097168 | tf_op jit(solution)/shard_map/all_gather | solution.py:111
  49.0 7.2 %convert_bitcast_fusion = bf16[4096,1024]{0,1:T(8,128)(2,1)} fusion(bf16[256,1024]{1,0:T(8,128)(2,1)S(1)} %bitcast_dynamic-update-slice_fusion, bf16[1,256,4096]{2,1,0:T(8,128)(2,1)} %all-gather.2.cloned.1.call-done), kind=kOutput, calls=%fused_computation.1 | convolution fusion | flops 2151677952 | bytes 11010048 | tf_op jit(solution)/shard_map/dot_general | solution.py:113
  56.2 12.0 %copy.54 = bf16[4096,1024]{1,0:T(8,128)(2,1)} copy(bf16[4096,1024]{0,1:T(8,128)(2,1)} %convert_bitcast_fusion) | data formatting | bytes 16777216
  68.1 0.0 reduce-scatter.7.cloned.1.call-update
  68.2 0.2 reduce-scatter.5.cloned.1.call-start
  68.4 9.3 %copy.62 = bf16[512,8,2,512]{3,1,2,0:T(8,128)(2,1)} copy(bf16[512,8,2,512]{3,2,1,0:T(2,128)(2,1)} %bitcast.28) | data formatting | bytes 16777216
  77.7 7.1 %convolution_convert_fusion = bf16[256,4096]{1,0:T(8,128)(2,1)} fusion(bf16[256,1024]{1,0:T(8,128)(2,1)S(1)} %bitcast_dynamic-update-slice_fusion, bf16[4096,1024]{1,0:T(8,128)(2,1)} %bitcast.29), kind=kOutput, calls=%fused_computation.2 | convolution fusion | flops 2148532224 | bytes 11010048 | tf_op jit(solution)/shard_map/dot_general | solution.py:103
  84.9 160.5 %reduce-scatter.7.cloned.1.call-done = bf16[128,1024]{1,0:T(8,128)(2,1)} async-done(((bf16[4096,1024]{1,0:T(8,128)(2,1)}), bf16[128,1024]{1,0:T(8,128)(2,1)}) %reduce-scatter.7.cloned.1.call-update) | async-done | bytes 262160
  245.3 1.1 copy.55
  246.5 1.0 copy.47
  247.5 47.0 %reduce-scatter.5.cloned.1.call-done = bf16[32,4096]{1,0:T(8,128)(2,1)} async-done(((bf16[256,4096]{1,0:T(8,128)(2,1)}), bf16[32,4096]{1,0:T(8,128)(2,1)}) %reduce-scatter.5.cloned.1.call-update) | async-done | bytes 262160 | tf_op jit(solution)/shard_map/reduce_scatter | solution.py:102
  (7 shorter events, 0.1 us)
Async XLA Ops:
  7.2 41.8 %all-gather.2.cloned.1.call-start = ((), (), s32[]{:S(2)}) async-start(), calls=%async_computation.3 | async-start | bytes 2359296 | tf_op jit(solution)/shard_map/all_gather | solution.py:111
  7.9 237.4 %reduce-scatter.7.cloned.1.call-start = ((), (), s32[]{:S(2)}) async-start(), calls=%async_computation.4 | async-start | bytes 8650752
  68.2 226.3 %reduce-scatter.5.cloned.1.call-start = ((), (), s32[]{:S(2)}) async-start(), calls=%async_computation.2 | async-start | bytes 2359296 | tf_op jit(solution)/shard_map/reduce_scatter | solution.py:102
Sparse Core Ops, SparseCore 0:
  9.8 39.0 all-gather.1
  68.3 176.9 reduce-scatter.6
  248.5 46.0 reduce-scatter.4
where the time goes:
time: 302 us; the launch traced here: 301 us
  waiting for transfers between devices  240 us (79%)
  local copies, waits for them, and re-layouts  28.7 us (10%)
  matrix products  15.8 us (5%)
  between operations  13.9 us (5%)
    unnamed x4, waiting for transfers between devices  161 us
    reduce_scatter x1, waiting for transfers between devices, shards(): lax.psum_scatter(lax.dot_general(grad_pair, weight_flat, (((1,), (1,)), (...  47 us
    all_gather x1, waiting for transfers between devices, shards(): gathered = lax.all_gather(layer_input, 'tensor', axis=1, tiled=True)[0]  31.7 us
    unnamed x5, local copies, waits for them, and re-layouts  23.4 us
    dot_general x1, matrix products, shards(): lax.dot_general(gathered, grad_pair, (((0,), (0,)), ((), ())), preferred_...  7.19 us
    dot_general x1, matrix products, shards(): lax.dot_general(grad_pair, weight_flat, (((1,), (1,)), ((), ())), preferr...  7.14 us
  transfers between devices with their start and end apart: 3, of which 3 were waited for; matrix products, arithmetic and copies ran while one was open for 9% of the time, Pallas kernels for 0%

commit v1 on v0

--- a/solution.py
+++ b/solution.py
@@ -6,6 +6,11 @@
 
 HD = 128
 SEQ = 128
+
+
+def swapped_in(x, mesh_axis, d):
+    repeated = jnp.stack([x] * lax.axis_size(mesh_axis))
+    return jnp.concatenate(lax.all_to_all(repeated, mesh_axis, 0, 0), axis=d)
 
 
 def rotate_pairs(values, cosine, sine_table):
@@ -108,7 +113,7 @@
         tiled=True,
     )
     input_grad = summed_input.reshape(1, token_count // tensor_count, model_width)
-    gathered = lax.all_gather(layer_input, "tensor", axis=1, tiled=True)[0]
+    gathered = swapped_in(layer_input, "tensor", 1)[0]
     summed = lax.psum_scatter(
         lax.dot_general(
             gathered, grad_pair, (((0,), (0,)), ((), ())), preferred_element_type=jnp.float32

time: 302 us -> 320 us (1.060)
  starting transfers between devices: 0.3 us -> 8.72 us
  waiting for transfers between devices: 240 us -> 244 us
    all_to_all x0 -> x1, waiting for transfers between devices: none -> 38.3 us  [swapped_in(): return jnp.concatenate(lax.all_to_all(repeated, mesh_axis, 0, 0), axis=d)]
    all_gather x1 -> x0, waiting for transfers between devices: 31.7 us -> none  [shards(): gathered = lax.all_gather(layer_input, 'tensor', axis=1, tiled=True)[0]]
    all_to_all x0 -> x1, starting transfers between devices: none -> 8.47 us  [swapped_in(): return jnp.concatenate(lax.all_to_all(repeated, mesh_axis, 0, 0), axis=d)]
    unnamed x4 -> x3, waiting for transfers between devices: 161 us -> 159 us
    unnamed x5 -> x11, local copies, waits for them, and re-layouts: 23.4 us -> 23.5 us
  transfers between devices with their start and end apart: 3 -> 3, of which waited for: 3 -> 3; matrix products, arithmetic and copies ran while one was open for 9% -> 10% of each run, Pallas kernels for 0% -> 0%
where the time goes in v1:
time: 320 us; the launch traced here: 319 us
  waiting for transfers between devices  244 us (76%)
  local copies, waits for them, and re-layouts  31.8 us (10%)
  matrix products  16.8 us (5%)
  between operations  14.2 us (4%)
  starting transfers between devices  8.72 us (3%)
  other arithmetic  3.27 us (1%)
    unnamed x3, waiting for transfers between devices  159 us
    reduce_scatter x1, waiting for transfers between devices, shards(): lax.psum_scatter(lax.dot_general(grad_pair, weight_flat, (((1,), (1,)), (...  47.3 us
    all_to_all x1, waiting for transfers between devices, swapped_in(): return jnp.concatenate(lax.all_to_all(repeated, mesh_axis, 0, 0), axis=d)  38.3 us
    unnamed x11, local copies, waits for them, and re-layouts  23.5 us
    all_to_all x1, starting transfers between devices, swapped_in(): return jnp.concatenate(lax.all_to_all(repeated, mesh_axis, 0, 0), axis=d)  8.47 us
    dot_general x1, matrix products, shards(): lax.dot_general(grad_pair, weight_flat, (((1,), (1,)), ((), ())), preferr...  7.11 us
  transfers between devices with their start and end apart: 3, of which 3 were waited for; matrix products, arithmetic and copies ran while one was open for 10% of the time, Pallas kernels for 0%

profile of v1, /device:TPU:8, one launch (start us, length us, event | category | flops | bytes accessed | tf_op | source)
XLA Modules:
  0.0 319.3 jit_solution(17610878486404545350)
XLA Ops:
  7.2 2.6 stack.2
  9.8 8.5 %all-to-all-start = ((bf16[8,1,32,4096]{3,2,1,0:T(8,128)(2,1)}), bf16[8,1,32,4096]{3,2,1,0:T(8,128)(2,1)S(1)}, u32[]{:S(2)}, u32[]{:S(2)}) async-start(bf16[8,1,32,4096]{3,2,1,0:T(8,128)(2,1)} %stack.2), calls=%async_computation.1 | async-start | bytes 4194304 | tf_op jit(solution)/shard_map/all_to_all | solution.py:13
  18.2 0.0 reduce-scatter.7.cloned.1.call-start
  18.3 1.1 reshape.113
  19.4 1.1 reshape.114
  20.5 1.7 reshape_squeeze.9
  22.2 0.8 reshape_squeeze.8
  23.1 0.7 compare_and_fusion
  23.8 0.3 multiply_cosine_fusion
  24.1 0.6 fusion.17
  24.7 0.3 subtract_convert_fusion.3
  25.0 2.0 fusion.19
  27.0 1.4 multiply_reduce_fusion
  28.5 1.1 multiply_convert_fusion
  29.6 0.3 fusion.3
  29.9 0.4 fusion.4
  30.3 0.5 add_convert_fusion
  30.7 0.1 pad_maximum_fusion.2
  30.9 0.2 copy.42
  31.1 0.1 pad_maximum_fusion.3
  31.3 0.2 copy.46
  31.6 38.3 %all-to-all-done = bf16[8,1,32,4096]{3,2,1,0:T(8,128)(2,1)S(1)} async-done(((bf16[8,1,32,4096]{3,2,1,0:T(8,128)(2,1)}), bf16[8,1,32,4096]{3,2,1,0:T(8,128)(2,1)S(1)}, u32[]{:S(2)}, u32[]{:S(2)}) %all-to-all-start) | async-done | bytes 2097184 | tf_op jit(solution)/shard_map/all_to_all | solution.py:13
  69.9 5.6 %convert_bitcast_fusion = bf16[4096,1024]{0,1:T(8,128)(2,1)} fusion(bf16[256,1024]{1,0:T(8,128)(2,1)S(1)} %bitcast_dynamic-update-slice_fusion, bf16[256,4096]{1,0:T(8,128)(2,1)S(1)} %bitcast.30), kind=kOutput, calls=%fused_computation.1 | convolution fusion | flops 2151677952 | bytes 11010048 | tf_op jit(solution)/shard_map/dot_general | solution.py:118
  75.5 12.0 %copy.54 = bf16[4096,1024]{1,0:T(8,128)(2,1)} copy(bf16[4096,1024]{0,1:T(8,128)(2,1)} %convert_bitcast_fusion) | data formatting | bytes 16777216
  87.5 0.0 reduce-scatter.7.cloned.1.call-update
  87.5 0.2 reduce-scatter.5.cloned.1.call-start
  87.7 9.3 %copy.62 = bf16[512,8,2,512]{3,1,2,0:T(8,128)(2,1)} copy(bf16[512,8,2,512]{3,2,1,0:T(2,128)(2,1)} %bitcast.28) | data formatting | bytes 16777216
  97.0 7.1 %convolution_convert_fusion = bf16[256,4096]{1,0:T(8,128)(2,1)} fusion(bf16[256,1024]{1,0:T(8,128)(2,1)S(1)} %bitcast_dynamic-update-slice_fusion, bf16[4096,1024]{1,0:T(8,128)(2,1)} %bitcast.29), kind=kOutput, calls=%fused_computation.2 | convolution fusion | flops 2148532224 | bytes 11010048 | tf_op jit(solution)/shard_map/dot_general | solution.py:108
  104.2 158.8 %reduce-scatter.7.cloned.1.call-done = bf16[128,1024]{1,0:T(8,128)(2,1)} async-done(((bf16[4096,1024]{1,0:T(8,128)(2,1)}), bf16[128,1024]{1,0:T(8,128)(2,1)}) %reduce-scatter.7.cloned.1.call-update) | async-done | bytes 262160
  263.0 1.1 copy.55
  264.1 1.0 copy.47
  265.1 47.3 %reduce-scatter.5.cloned.1.call-done = bf16[32,4096]{1,0:T(8,128)(2,1)} async-done(((bf16[256,4096]{1,0:T(8,128)(2,1)}), bf16[32,4096]{1,0:T(8,128)(2,1)}) %reduce-scatter.5.cloned.1.call-update) | async-done | bytes 262160 | tf_op jit(solution)/shard_map/reduce_scatter | solution.py:107
  (13 shorter events, 0.2 us)
Async XLA Ops:
  7.2 15.1 %copy-start = (bf16[1,256,512]{2,1,0:T(8,128)(2,1)S(1)}, bf16[1,256,512]{2,1,0:T(8,128)(2,1)}, u32[]{:S(2)}) copy-start(bf16[1,256,512]{2,1,0:T(8,128)(2,1)} %param.12) | copy-start | bytes 786436
  7.2 15.9 %copy-start.2 = (s32[1,256]{1,0:T(1,128)S(1)}, s32[1,256]{1,0:T(1,128)}, u32[]{:S(2)}) copy-start(s32[1,256]{1,0:T(1,128)} %param.13) | copy-start | bytes 3076
  9.8 60.1 %all-to-all-start = ((bf16[8,1,32,4096]{3,2,1,0:T(8,128)(2,1)}), bf16[8,1,32,4096]{3,2,1,0:T(8,128)(2,1)S(1)}, u32[]{:S(2)}, u32[]{:S(2)}) async-start(bf16[8,1,32,4096]{3,2,1,0:T(8,128)(2,1)} %stack.2), calls=%async_computation.1 | async-start | bytes 4194304 | tf_op jit(solution)/shard_map/all_to_all | solution.py:13
  18.2 244.8 %reduce-scatter.7.cloned.1.call-start = ((), (), s32[]{:S(2)}) async-start(), calls=%async_computation.4 | async-start | bytes 8650752
  23.0 4.0 %copy-start.1 = (bf16[2,128,4,128]{3,2,1,0:T(4,128)(2,1)S(1)}, bf16[2,128,4,128]{3,2,1,0:T(4,128)(2,1)}, u32[]{:S(2)}) copy-start(bf16[2,128,4,128]{3,2,1,0:T(4,128)(2,1)} %reshape_squeeze.9) | copy-start | bytes 786436
  87.5 224.9 %reduce-scatter.5.cloned.1.call-start = ((), (), s32[]{:S(2)}) async-start(), calls=%async_computation.3 | async-start | bytes 2359296 | tf_op jit(solution)/shard_map/reduce_scatter | solution.py:107
Sparse Core Ops, SparseCore 0:
  87.6 175.3 reduce-scatter.6
  266.1 46.2 reduce-scatter.4
